TPU v7x, 32 devices: a whole 2x2x4 slice. The times are simulated.
32 devices in a mesh: tm: 4 (over x, core), row: 2 (over y), col: 4 (over z).
Axes of the slice: x: 2, y: 2, z: 4, core: 2. Of those that a mesh axis runs over, the one named last changes fastest.
Arguments:
- first_inverse: bfloat16 [4, 1536, 1536], P('tm', ('row', 'col')), as said below
- second_diag: bfloat16 [4, 1536, 1536], P('tm', ('row', 'col')), as said below
- coupling: bfloat16 [4, 3, 1536, 1536], P('tm', None, ('row', 'col'))
- arrow_rows: float32 [4, 2, 8, 1536], P('tm')
- tip_block: float32 [8, 8], replicated, may hold values from -6 to 6
Outputs:
- separator_update: float32 [4, 1536, 1536], P('tm', ('row', 'col'))
- separator_fill: float32 [4, 1536, 1536], P('tm', ('row', 'col'))
- reduced_tip: float32 [8, 8], replicated
Inputs may be any that keep to these rules, and one draw needn't show every extreme that they name: For every p, first_inverse[p] is lower triangular with a positive diagonal. For every p, second_diag[p] is symmetric, and second_diag[p] minus coupling[p, 1] first_inverse[p]^T first_inverse[p] coupling[p, 1]^T is positive definite.
All inputs are finite; a program needn't handle non-finite values.
Results may differ from a plain program's by a relative error of at most 0.009.
Values may be sent and summed in bfloat16 or wider, within the bound.
No kernel may reach another device: no remote copies, remote signals or barrier semaphores. Data moves between devices by JAX's collectives and lax.ppermute only.
A program may use at most 128 MiB of HBM per device.

v0:
```python
import jax
import jax.numpy as jnp
from jax import lax
from jax.sharding import PartitionSpec as P


def from_behind(block, axis, distance):
    devices = range(lax.axis_size(axis))
    route = [(i - distance, i) for i in devices if i - distance in devices]
    return lax.ppermute(block, axis, route)


def right_solve(factor, rhs_rows):
    return lax.linalg.triangular_solve(
        factor, rhs_rows, left_side=False, lower=True, transpose_a=True
    )


def outer_rows(left_rows, right_rows):
    return jnp.einsum("ik,jk->ij", left_rows, right_rows, preferred_element_type=jnp.float32)


def gather_block(one_share):
    return lax.all_gather(one_share, ("row", "col"), axis=0, tiled=True)


def spread_panels(first_panel, second_panel):
    return (
        lax.all_gather(first_panel, ("row", "col"), axis=0, tiled=True),
        lax.all_gather(second_panel, ("row", "col"), axis=0, tiled=True),
    )


def shards(first_inverse, second_diag, coupling, arrow_rows, tip_block):
    share = coupling.shape[2]
    inverse_whole = gather_block(first_inverse[0])
    rhs_first = jnp.concatenate([coupling[0, 0], coupling[0, 1]], axis=0)
    solved_first = outer_rows(rhs_first, inverse_whole)
    top_own = solved_first[:share].astype(jnp.bfloat16)
    mid_own = solved_first[share:].astype(jnp.bfloat16)
    arrow_one = jnp.einsum(
        "ik,jk->ij",
        arrow_rows[0, 0],
        inverse_whole.astype(jnp.float32),
        precision=lax.Precision.HIGHEST,
    )
    top_whole, mid_whole = spread_panels(top_own, mid_own)
    sep_first = outer_rows(top_own, top_whole)
    fill_rows = -outer_rows(top_own, mid_whole)
    arrow_two_rows = arrow_rows[0, 1] - outer_rows(arrow_one.astype(jnp.bfloat16), mid_whole)
    tip_first = jnp.einsum("ik,jk->ij", arrow_one, arrow_one, precision=lax.Precision.HIGHEST)
    second_share = (second_diag[0].astype(jnp.float32) - outer_rows(mid_own, mid_whole)).astype(
        jnp.bfloat16
    )
    second_ready = gather_block(second_share)
    factor_two = jnp.linalg.cholesky(second_ready.astype(jnp.float32))
    rhs_second = jnp.concatenate(
        [fill_rows, coupling[0, 2].astype(jnp.float32), arrow_two_rows], axis=0
    )
    solved_second = right_solve(factor_two, rhs_second)
    upper_own = solved_second[:share].astype(jnp.bfloat16)
    lower_own = solved_second[share : 2 * share].astype(jnp.bfloat16)
    arrow_two = solved_second[2 * share :]
    tip_second = jnp.einsum("ik,jk->ij", arrow_two, arrow_two, precision=lax.Precision.HIGHEST)
    upper_whole, lower_whole = spread_panels(upper_own, lower_own)
    sep_second = outer_rows(upper_own, upper_whole)
    fill_block = -outer_rows(upper_own, lower_whole)
    handed = outer_rows(lower_own, lower_whole)
    incoming = from_behind(handed, "tm", 1)
    tip_total = lax.psum(tip_first + tip_second, "tm")
    separator_update = sep_first + sep_second + incoming
    return (separator_update[None], fill_block[None], tip_block - tip_total)


def solution(mesh):
    return jax.shard_map(
        shards,
        mesh=mesh,
        in_specs=(
            P("tm", ("row", "col"), None),
            P("tm", ("row", "col"), None),
            P("tm", None, ("row", "col"), None),
            P("tm", None, None, None),
            P(),
        ),
        out_specs=(P("tm", ("row", "col"), None), P("tm", ("row", "col"), None), P()),
        check_vma=False,
    )
```

profile of v0, /device:TPU:0, one launch (start us, length us, event | category | flops | bytes accessed | tf_op | source)
XLA Modules:
  0.0 1064.2 jit_solution(15958643128094356016)
XLA Ops:
  9.5 82.6 %all-gather.18.cloned.1.call-done = bf16[1,1536,1536]{2,1,0:T(8,128)(2,1)} async-done(((bf16[1,192,1536]{2,1,0:T(8,128)(2,1)}), bf16[1,1536,1536]{2,1,0:T(8,128)(2,1)}) %all-gather.18.cloned.1.call-update) | async-done | bytes 4718608 | tf_op jit(solution)/shard_map/all_gather | solution.py:24
  92.2 4.4 fusion.5
  97.7 77.8 %all-gather.10.cloned.1.call-done = bf16[1536,1536]{1,0:T(8,128)(2,1)} async-done(((bf16[192,1536]{1,0:T(8,128)(2,1)}), bf16[1536,1536]{1,0:T(8,128)(2,1)}) %all-gather.10.cloned.1.call-update) | async-done | bytes 4718608 | tf_op jit(solution)/shard_map/all_gather | solution.py:30
  175.5 4.8 fusion.11
  180.4 6.2 fusion.1
  191.3 66.9 %all-gather.12.cloned.1.call-done = bf16[1536,1536]{1,0:T(8,128)(2,1)} async-done(((bf16[192,1536]{1,0:T(8,128)(2,1)}), bf16[1536,1536]{1,0:T(8,128)(2,1)}) %all-gather.12.cloned.1.call-update) | async-done | bytes 4718608 | tf_op jit(solution)/shard_map/all_gather | solution.py:24
  258.2 6.6 copy.11
  264.8 7.9 copy.12
  272.8 6.5 fusion
  279.3 3.6 copy-done
  282.9 11.7 %cholesky.341 = f32[128,128]{1,0:T(8,128)S(1)} custom-call(f32[128,128]{1,0:T(8,128)S(1)} %cholesky.892), custom_call_target="Cholesky" | custom-call | tf_op jit(solution)/shard_map/jit(cholesky)/cholesky | solution.py:56
  294.7 9.8 custom-call.94
  304.5 4.8 cholesky.371
  314.0 11.9 %cholesky.362 = f32[128,128]{1,0:T(8,128)S(1)} custom-call(f32[128,128]{1,0:T(8,128)S(1)} %cholesky.896), custom_call_target="Cholesky" | custom-call | tf_op jit(solution)/shard_map/jit(cholesky)/cholesky | solution.py:56
  326.5 9.8 custom-call.95
  340.7 11.7 %cholesky.385 = f32[128,128]{1,0:T(8,128)S(1)} custom-call(f32[128,128]{1,0:T(8,128)S(1)} %cholesky.901), custom_call_target="Cholesky" | custom-call | tf_op jit(solution)/shard_map/jit(cholesky)/cholesky | solution.py:56
  353.7 9.8 custom-call.96
  368.6 11.7 %cholesky.715 = f32[128,128]{1,0:T(8,128)S(1)} custom-call(f32[128,128]{1,0:T(8,128)S(1)} %cholesky.906), custom_call_target="Cholesky" | custom-call | tf_op jit(solution)/shard_map/jit(cholesky)/cholesky | solution.py:56
  381.6 9.8 custom-call.97
  396.5 12.1 %cholesky.734 = f32[128,128]{1,0:T(8,128)S(1)} custom-call(f32[128,128]{1,0:T(8,128)S(1)} %cholesky.911), custom_call_target="Cholesky" | custom-call | tf_op jit(solution)/shard_map/jit(cholesky)/cholesky | solution.py:56
  409.9 9.8 custom-call.98
  421.1 3.8 fusion.31
  424.9 11.7 %cholesky.754 = f32[128,128]{1,0:T(8,128)S(1)} custom-call(f32[128,128]{1,0:T(8,128)S(1)} %cholesky.916), custom_call_target="Cholesky" | custom-call | tf_op jit(solution)/shard_map/jit(cholesky)/cholesky | solution.py:56
  438.0 9.9 custom-call.99
  449.2 3.8 fusion.34
  453.0 11.7 %cholesky.774 = f32[128,128]{1,0:T(8,128)S(1)} custom-call(f32[128,128]{1,0:T(8,128)S(1)} %cholesky.921), custom_call_target="Cholesky" | custom-call | tf_op jit(solution)/shard_map/jit(cholesky)/cholesky | solution.py:56
  466.1 9.8 custom-call.100
  477.1 3.8 fusion.37
  480.9 11.9 %cholesky.794 = f32[128,128]{1,0:T(8,128)S(1)} custom-call(f32[128,128]{1,0:T(8,128)S(1)} %cholesky.926), custom_call_target="Cholesky" | custom-call | tf_op jit(solution)/shard_map/jit(cholesky)/cholesky | solution.py:56
  494.2 9.8 custom-call.101
  508.7 11.7 %cholesky.814 = f32[128,128]{1,0:T(8,128)S(1)} custom-call(f32[128,128]{1,0:T(8,128)S(1)} %cholesky.931), custom_call_target="Cholesky" | custom-call | tf_op jit(solution)/shard_map/jit(cholesky)/cholesky | solution.py:56
  521.7 10.2 custom-call.102
  536.3 11.7 %cholesky.834 = f32[128,128]{1,0:T(8,128)S(1)} custom-call(f32[128,128]{1,0:T(8,128)S(1)} %cholesky.936), custom_call_target="Cholesky" | custom-call | tf_op jit(solution)/shard_map/jit(cholesky)/cholesky | solution.py:56
  549.3 9.8 custom-call.103
  562.9 11.9 %cholesky.854 = f32[128,128]{1,0:T(8,128)S(1)} custom-call(f32[128,128]{1,0:T(8,128)S(1)} %cholesky.941), custom_call_target="Cholesky" | custom-call | tf_op jit(solution)/shard_map/jit(cholesky)/cholesky | solution.py:56
  576.1 9.8 custom-call.104
  589.0 11.7 %cholesky.872 = f32[128,128]{1,0:T(8,128)S(1)} custom-call(f32[128,128]{1,0:T(8,128)S(1)} %convolution_subtract_fusion.16), custom_call_target="Cholesky" | custom-call | tf_op jit(solution)/shard_map/jit(cholesky)/cholesky | solution.py:56
  610.4 8.6 select_select_fusion
  619.0 43.1 %while.1 = (s32[]{:T(128)}, f32[1536,1536]{1,0:T(8,128)}, s32[12,2]{0,1:T(2,128)S(1)}, f32[12,128,128]{2,1,0:T(8,128)}, s32[]{:T(128)}) while((s32[]{:T(128)}, f32[1536,1536]{1,0:T(8,128)}, s32[12,2]{0,1:T(2,128)S(1)}, f32[12,128,128]{2,1,0:T(8,128)}, s32[]{:T(128)}) %tuple.111), condition=%wide.while_cond, body=%wide.while_body.sunk | while | flops 2 | bytes 132205 | solution.py:14
  662.1 119.7 %custom-call.105 = f32[12,128,128]{1,2,0:T(8,128)} custom-call(f32[12,128,128]{2,1,0:T(8,128)} %get-tuple-element.10), custom_call_target="InvertDiagBlocksLowerTriangular" | custom-call | tf_op jit(solution)/shard_map/triangular_solve | solution.py:14
  815.8 76.7 %all-gather.16.cloned.1.call-done = bf16[1536,1536]{1,0:T(8,128)(2,1)} async-done(((bf16[192,1536]{1,0:T(8,128)(2,1)}), bf16[1536,1536]{1,0:T(8,128)(2,1)}) %all-gather.16.cloned.1.call-update) | async-done | bytes 4718608 | tf_op jit(solution)/shard_map/all_gather | solution.py:30
  892.5 5.0 fusion.132
  899.0 73.1 %all-gather.8.cloned.1.call-done = bf16[1536,1536]{1,0:T(8,128)(2,1)} async-done(((bf16[192,1536]{1,0:T(8,128)(2,1)}), bf16[1536,1536]{1,0:T(8,128)(2,1)}) %all-gather.8.cloned.1.call-update) | async-done | bytes 4718608 | tf_op jit(solution)/shard_map/all_gather | solution.py:29
  972.1 5.2 fusion.138
  978.4 5.7 psum.7
  984.7 5.0 fusion.8
  989.7 62.1 %all-gather.14.cloned.1.call-done = bf16[1536,1536]{1,0:T(8,128)(2,1)} async-done(((bf16[192,1536]{1,0:T(8,128)(2,1)}), bf16[1536,1536]{1,0:T(8,128)(2,1)}) %all-gather.14.cloned.1.call-update) | async-done | bytes 4718608 | tf_op jit(solution)/shard_map/all_gather | solution.py:29
  1051.8 5.4 fusion.10
  (156 shorter events, 141.7 us)
Async XLA Ops:
  7.2 85.0 %all-gather.18.cloned.1.call-start = ((), (), s32[]{:S(2)}) async-start(), calls=%async_computation.5 | async-start | bytes 5308416 | tf_op jit(solution)/shard_map/all_gather | solution.py:24
  7.9 167.6 %all-gather.10.cloned.1.call-start = ((), (), s32[]{:S(2)}) async-start(), calls=%async_computation.1 | async-start | bytes 5308416 | tf_op jit(solution)/shard_map/all_gather | solution.py:30
  96.5 91.5 %copy-start.4 = (bf16[384,1536]{1,0:T(8,128)(2,1)}, bf16[384,1536]{1,0:T(8,128)(2,1)S(1)}, u32[]{:S(2)}) copy-start(bf16[384,1536]{1,0:T(8,128)(2,1)S(1)} %fusion.5) | copy-start | bytes 3538948
  96.5 79.0 %copy-start.8 = (bf16[1,192,1536]{2,1,0:T(8,128)(2,1)S(1)}, bf16[1,192,1536]{2,1,0:T(8,128)(2,1)}, u32[]{:S(2)}) copy-start(bf16[1,192,1536]{2,1,0:T(8,128)(2,1)} %param.6) | copy-start | bytes 1769476
  97.7 82.8 %copy-start.6 = (f32[1,2,8,1536]{3,2,1,0:T(8,128)S(1)}, f32[1,2,8,1536]{3,2,1,0:T(8,128)}, u32[]{:S(2)}) copy-start(f32[1,2,8,1536]{3,2,1,0:T(8,128)} %param.8) | copy-start | bytes 294916
  97.7 160.5 %all-gather.12.cloned.1.call-start = ((), (), s32[]{:S(2)}) async-start(), calls=%async_computation.2 | async-start | bytes 5308416 | tf_op jit(solution)/shard_map/all_gather | solution.py:24
  180.4 712.1 %all-gather.16.cloned.1.call-start = ((), (), s32[]{:S(2)}) async-start(), calls=%async_computation.4 | async-start | bytes 5308416 | tf_op jit(solution)/shard_map/all_gather | solution.py:30
  180.4 6.2 copy-start.2
  279.3 3.6 copy-start
  610.4 171.4 %copy-start.1 = (f32[392,1536]{1,0:T(8,128)S(1)}, f32[392,1536]{1,0:T(8,128)}, u32[]{:S(2)}) copy-start(f32[392,1536]{1,0:T(8,128)} %pad_maximum_fusion) | copy-start | bytes 7225348
  781.8 2.8 copy-start.5
  812.8 1.8 copy-start.3
  814.6 157.5 %all-gather.8.cloned.1.call-start = ((), (), s32[]{:S(2)}) async-start(), calls=%async_computation | async-start | bytes 5308416 | tf_op jit(solution)/shard_map/all_gather | solution.py:29
  815.2 236.6 %all-gather.14.cloned.1.call-start = ((), (), s32[]{:S(2)}) async-start(), calls=%async_computation.3 | async-start | bytes 5308416 | tf_op jit(solution)/shard_map/all_gather | solution.py:29
  897.5 154.3 %collective-permute-start = (f32[192,1536]{1,0:T(8,128)}, f32[192,1536]{1,0:T(8,128)S(1)}, u32[]{:S(2)}, u32[]{:S(2)}) collective-permute-start(f32[192,1536]{1,0:T(8,128)} %fusion.132), channel_id=1, source_target_pairs={{0,8},{8,16},{16,24},{1,9},{9,17},{17,25},{2,10},{10,18},{18,26},{... | collective-permute-start | bytes 3538952 | tf_op jit(solution)/shard_map/ppermute | solution.py:10
  899.0 85.1 %copy-start.7 = (f32[8,8]{1,0:T(8,128)S(1)}, f32[8,8]{1,0:T(8,128)}, u32[]{:S(2)}) copy-start(f32[8,8]{1,0:T(8,128)} %param.9) | copy-start | bytes 772
Sparse Core Ops, SparseCore 0:
  10.1 82.0 all-gather.17
  97.8 77.6 all-gather.9
  180.5 77.6 all-gather.11
  814.7 77.6 all-gather.15
  894.4 77.6 all-gather.7
  974.1 77.6 all-gather.13
where the time goes:
time: 1070 us; the launch traced here: 1060 us
  waiting for transfers between devices  441 us (41%)
  other arithmetic  403 us (38%)
  matrix products  121 us (11%)
  local copies, waits for them, and re-layouts  68.9 us (6%)
  between operations  22.4 us (2%)
    another operation x46, other arithmetic, shards(): factor_two = jnp.linalg.cholesky(second_ready.astype(jnp.float32))  265 us
    all_gather x2, waiting for transfers between devices, spread_panels(): lax.all_gather(second_panel, ('row', 'col'), axis=0, tiled=True)  154 us
    all_gather x2, waiting for transfers between devices, gather_block(): return lax.all_gather(one_share, ('row', 'col'), axis=0, tiled=True)  150 us
    all_gather x2, waiting for transfers between devices, spread_panels(): lax.all_gather(first_panel, ('row', 'col'), axis=0, tiled=True)  135 us
    another operation x3, other arithmetic, right_solve(): lax.linalg.triangular_solve(factor, rhs_rows, left_side=False, lower=True...  128 us
    another operation x22, matrix products, shards(): factor_two = jnp.linalg.cholesky(second_ready.astype(jnp.float32))  50.1 us
    another operation x36, local copies, waits for them, and re-layouts  43 us
    dot_general x8, matrix products, outer_rows(): jnp.einsum('ik,jk->ij', left_rows, right_rows, preferred_element_type=jnp...  32.9 us
  transfers between devices with their start and end apart: 7, of which 6 were waited for; matrix products, arithmetic and copies ran while one was open for 3% of the time, Pallas kernels for 0%

commit v1 on v0

--- a/solution.py
+++ b/solution.py
@@ -2,6 +2,17 @@
 import jax.numpy as jnp
 from jax import lax
 from jax.sharding import PartitionSpec as P
+
+
+def collect(value, axis, dim):
+    ways = lax.axis_size(axis)
+    pieces = [value]
+    for far in range(1, ways):
+        pieces.append(
+            lax.ppermute(pieces[far - 1], axis, [(d, (d - 1) % ways) for d in range(ways)])
+        )
+    line = jnp.concatenate(pieces, axis=dim)
+    return jnp.roll(line, lax.axis_index(axis) * value.shape[dim], axis=dim)
 
 
 def from_behind(block, axis, distance):
@@ -27,7 +38,7 @@
 def spread_panels(first_panel, second_panel):
     return (
         lax.all_gather(first_panel, ("row", "col"), axis=0, tiled=True),
-        lax.all_gather(second_panel, ("row", "col"), axis=0, tiled=True),
+        collect(second_panel, ("row", "col"), 0),
     )
 
 

time: 1070 us -> 1070 us (level)
  waiting for transfers between devices: 441 us -> 352 us
  starting transfers between devices: 1.59 us -> 54 us
  local copies, waits for them, and re-layouts: 68.9 us -> 86.4 us
  other arithmetic: 403 us -> 419 us
    ppermute x0 -> x14, waiting for transfers between devices: none -> 199 us  [collect(): lax.ppermute(pieces[far - 1], axis, [(d, (d - 1) % ways) for d in range(w...]
    all_gather x2 -> x0, waiting for transfers between devices: 154 us -> none  [spread_panels(): lax.all_gather(second_panel, ('row', 'col'), axis=0, tiled=True)]
    all_gather x2, waiting for transfers between devices: 135 us -> 0.02 us  [spread_panels(): lax.all_gather(first_panel, ('row', 'col'), axis=0, tiled=True)]
    ppermute x0 -> x14, starting transfers between devices: none -> 51.9 us  [collect(): lax.ppermute(pieces[far - 1], axis, [(d, (d - 1) % ways) for d in range(w...]
    unnamed x18 -> x38, local copies, waits for them, and re-layouts: 3.96 us -> 19.5 us
    concatenate x0 -> x2, other arithmetic: none -> 14.2 us  [collect(): return jnp.roll(line, lax.axis_index(axis) * value.shape[dim], axis=dim)]
  transfers between devices with their start and end apart: 7 -> 19, of which waited for: 6 -> 16; matrix products, arithmetic and copies ran while one was open for 3% -> 56% of each run, Pallas kernels for 0% -> 0%
where the time goes in v1:
time: 1070 us; the launch traced here: 1060 us
  other arithmetic  419 us (39%)
  waiting for transfers between devices  352 us (33%)
  matrix products  116 us (11%)
  local copies, waits for them, and re-layouts  86.4 us (8%)
  starting transfers between devices  54 us (5%)
  between operations  22.1 us (2%)
    another operation x46, other arithmetic, shards(): factor_two = jnp.linalg.cholesky(second_ready.astype(jnp.float32))  265 us
    ppermute x14, waiting for transfers between devices, collect(): lax.ppermute(pieces[far - 1], axis, [(d, (d - 1) % ways) for d in range(w...  199 us
    all_gather x2, waiting for transfers between devices, gather_block(): return lax.all_gather(one_share, ('row', 'col'), axis=0, tiled=True)  152 us
    another operation x3, other arithmetic, right_solve(): lax.linalg.triangular_solve(factor, rhs_rows, left_side=False, lower=True...  128 us
    ppermute x14, starting transfers between devices, collect(): lax.ppermute(pieces[far - 1], axis, [(d, (d - 1) % ways) for d in range(w...  51.9 us
    another operation x22, matrix products, shards(): factor_two = jnp.linalg.cholesky(second_ready.astype(jnp.float32))  50.1 us
    another operation x36, local copies, waits for them, and re-layouts  43 us
    another operation x23, matrix products, right_solve(): lax.linalg.triangular_solve(factor, rhs_rows, left_side=False, lower=True...  31.1 us
  transfers between devices with their start and end apart: 19, of which 16 were waited for; matrix products, arithmetic and copies ran while one was open for 56% of the time, Pallas kernels for 0%

profile of v1, /device:TPU:0, one launch (start us, length us, event | category | flops | bytes accessed | tf_op | source)
XLA Modules:
  0.0 1056.5 jit_solution(4094758188513718265)
XLA Ops:
  9.5 82.6 %all-gather.12.cloned.1.call-done = bf16[1,1536,1536]{2,1,0:T(8,128)(2,1)} async-done(((bf16[1,192,1536]{2,1,0:T(8,128)(2,1)}), bf16[1,1536,1536]{2,1,0:T(8,128)(2,1)}) %all-gather.12.cloned.1.call-update) | async-done | bytes 4718608 | tf_op jit(solution)/shard_map/all_gather | solution.py:35
  99.5 12.6 %collective-permute-done = bf16[192,1536]{1,0:T(8,128)(2,1)S(1)} collective-permute-done((bf16[192,1536]{1,0:T(8,128)(2,1)S(1)}, bf16[192,1536]{1,0:T(8,128)(2,1)S(1)}, u32[]{:S(2)}, u32[]{:S(2)}) %collective-permute-start) | collective-permute-done | bytes 589856 | tf_op jit(solution)/shard_map/ppermute | solution.py:12
  117.3 11.8 %collective-permute-done.1 = bf16[192,1536]{1,0:T(8,128)(2,1)S(1)} collective-permute-done((bf16[192,1536]{1,0:T(8,128)(2,1)S(1)}, bf16[192,1536]{1,0:T(8,128)(2,1)S(1)}, u32[]{:S(2)}, u32[]{:S(2)}) %collective-permute-start.1) | collective-permute-done | bytes 589856 | tf_op jit(solution)/shard_map/ppermute | solution.py:12
  134.2 10.9 %collective-permute-done.2 = bf16[192,1536]{1,0:T(8,128)(2,1)S(1)} collective-permute-done((bf16[192,1536]{1,0:T(8,128)(2,1)S(1)}, bf16[192,1536]{1,0:T(8,128)(2,1)S(1)}, u32[]{:S(2)}, u32[]{:S(2)}) %collective-permute-start.2) | collective-permute-done | bytes 589856 | tf_op jit(solution)/shard_map/ppermute | solution.py:12
  151.1 10.0 collective-permute-done.3
  166.4 9.5 collective-permute-done.4
  183.7 6.1 collective-permute-done.5
  203.2 7.1 fusion.2
  216.4 6.2 fusion.3
  227.3 69.0 %all-gather.8.cloned.1.call-done = bf16[1536,1536]{1,0:T(8,128)(2,1)} async-done(((bf16[192,1536]{1,0:T(8,128)(2,1)}), bf16[1536,1536]{1,0:T(8,128)(2,1)}) %all-gather.8.cloned.1.call-update) | async-done | bytes 4718608 | tf_op jit(solution)/shard_map/all_gather | solution.py:35
  296.3 6.6 copy.11
  302.9 7.7 copy.12
  310.6 6.5 fusion
  320.8 11.7 %cholesky.341 = f32[128,128]{1,0:T(8,128)S(1)} custom-call(f32[128,128]{1,0:T(8,128)S(1)} %cholesky.892), custom_call_target="Cholesky" | custom-call | tf_op jit(solution)/shard_map/jit(cholesky)/cholesky | solution.py:67
  332.5 9.8 custom-call.94
  351.8 11.9 %cholesky.362 = f32[128,128]{1,0:T(8,128)S(1)} custom-call(f32[128,128]{1,0:T(8,128)S(1)} %cholesky.896), custom_call_target="Cholesky" | custom-call | tf_op jit(solution)/shard_map/jit(cholesky)/cholesky | solution.py:67
  364.4 9.8 custom-call.95
  378.5 11.7 %cholesky.385 = f32[128,128]{1,0:T(8,128)S(1)} custom-call(f32[128,128]{1,0:T(8,128)S(1)} %cholesky.901), custom_call_target="Cholesky" | custom-call | tf_op jit(solution)/shard_map/jit(cholesky)/cholesky | solution.py:67
  391.5 9.8 custom-call.96
  406.4 11.7 %cholesky.715 = f32[128,128]{1,0:T(8,128)S(1)} custom-call(f32[128,128]{1,0:T(8,128)S(1)} %cholesky.906), custom_call_target="Cholesky" | custom-call | tf_op jit(solution)/shard_map/jit(cholesky)/cholesky | solution.py:67
  419.4 9.8 custom-call.97
  434.3 12.1 %cholesky.734 = f32[128,128]{1,0:T(8,128)S(1)} custom-call(f32[128,128]{1,0:T(8,128)S(1)} %cholesky.911), custom_call_target="Cholesky" | custom-call | tf_op jit(solution)/shard_map/jit(cholesky)/cholesky | solution.py:67
  447.6 9.8 custom-call.98
  462.7 11.7 %cholesky.754 = f32[128,128]{1,0:T(8,128)S(1)} custom-call(f32[128,128]{1,0:T(8,128)S(1)} %cholesky.916), custom_call_target="Cholesky" | custom-call | tf_op jit(solution)/shard_map/jit(cholesky)/cholesky | solution.py:67
  475.8 9.9 custom-call.99
  490.8 11.7 %cholesky.774 = f32[128,128]{1,0:T(8,128)S(1)} custom-call(f32[128,128]{1,0:T(8,128)S(1)} %cholesky.921), custom_call_target="Cholesky" | custom-call | tf_op jit(solution)/shard_map/jit(cholesky)/cholesky | solution.py:67
  503.9 9.8 custom-call.100
  518.7 11.9 %cholesky.794 = f32[128,128]{1,0:T(8,128)S(1)} custom-call(f32[128,128]{1,0:T(8,128)S(1)} %cholesky.926), custom_call_target="Cholesky" | custom-call | tf_op jit(solution)/shard_map/jit(cholesky)/cholesky | solution.py:67
  532.0 9.8 custom-call.101
  546.5 11.7 %cholesky.814 = f32[128,128]{1,0:T(8,128)S(1)} custom-call(f32[128,128]{1,0:T(8,128)S(1)} %cholesky.931), custom_call_target="Cholesky" | custom-call | tf_op jit(solution)/shard_map/jit(cholesky)/cholesky | solution.py:67
  559.5 10.2 custom-call.102
  574.1 11.7 %cholesky.834 = f32[128,128]{1,0:T(8,128)S(1)} custom-call(f32[128,128]{1,0:T(8,128)S(1)} %cholesky.936), custom_call_target="Cholesky" | custom-call | tf_op jit(solution)/shard_map/jit(cholesky)/cholesky | solution.py:67
  587.1 9.8 custom-call.103
  600.7 11.9 %cholesky.854 = f32[128,128]{1,0:T(8,128)S(1)} custom-call(f32[128,128]{1,0:T(8,128)S(1)} %cholesky.941), custom_call_target="Cholesky" | custom-call | tf_op jit(solution)/shard_map/jit(cholesky)/cholesky | solution.py:67
  613.9 9.8 custom-call.104
  626.9 11.7 %cholesky.872 = f32[128,128]{1,0:T(8,128)S(1)} custom-call(f32[128,128]{1,0:T(8,128)S(1)} %convolution_subtract_fusion.5), custom_call_target="Cholesky" | custom-call | tf_op jit(solution)/shard_map/jit(cholesky)/cholesky | solution.py:67
  648.1 8.6 select_select_fusion
  656.8 43.1 %while.1 = (s32[]{:T(128)}, f32[1536,1536]{1,0:T(8,128)}, s32[12,2]{0,1:T(2,128)S(1)}, f32[12,128,128]{2,1,0:T(8,128)}, s32[]{:T(128)}) while((s32[]{:T(128)}, f32[1536,1536]{1,0:T(8,128)}, s32[12,2]{0,1:T(2,128)S(1)}, f32[12,128,128]{2,1,0:T(8,128)}, s32[]{:T(128)}) %tuple.114), condition=%wide.while_cond, body=%wide.while_body.sunk | while | flops 2 | bytes 132205 | solution.py:25
  699.8 119.5 %custom-call.105 = f32[12,128,128]{1,2,0:T(8,128)} custom-call(f32[12,128,128]{2,1,0:T(8,128)} %get-tuple-element.11), custom_call_target="InvertDiagBlocksLowerTriangular" | custom-call | tf_op jit(solution)/shard_map/triangular_solve | solution.py:25
  854.1 25.4 %collective-permute-done.7 = bf16[192,1536]{1,0:T(8,128)(2,1)S(1)} collective-permute-done((bf16[192,1536]{1,0:T(8,128)(2,1)S(1)}, bf16[192,1536]{1,0:T(8,128)(2,1)S(1)}, u32[]{:S(2)}, u32[]{:S(2)}) %collective-permute-start.7) | collective-permute-done | bytes 589856 | tf_op jit(solution)/shard_map/ppermute | solution.py:12
  879.8 18.5 %collective-permute-done.8 = bf16[192,1536]{1,0:T(8,128)(2,1)S(1)} collective-permute-done((bf16[192,1536]{1,0:T(8,128)(2,1)S(1)}, bf16[192,1536]{1,0:T(8,128)(2,1)S(1)}, u32[]{:S(2)}, u32[]{:S(2)}) %collective-permute-start.8) | collective-permute-done | bytes 589856 | tf_op jit(solution)/shard_map/ppermute | solution.py:12
  903.5 27.9 %collective-permute-done.9 = bf16[192,1536]{1,0:T(8,128)(2,1)S(1)} collective-permute-done((bf16[192,1536]{1,0:T(8,128)(2,1)S(1)}, bf16[192,1536]{1,0:T(8,128)(2,1)S(1)}, u32[]{:S(2)}, u32[]{:S(2)}) %collective-permute-start.9) | collective-permute-done | bytes 589856 | tf_op jit(solution)/shard_map/ppermute | solution.py:12
  932.9 29.9 %collective-permute-done.10 = bf16[192,1536]{1,0:T(8,128)(2,1)S(1)} collective-permute-done((bf16[192,1536]{1,0:T(8,128)(2,1)S(1)}, bf16[192,1536]{1,0:T(8,128)(2,1)S(1)}, u32[]{:S(2)}, u32[]{:S(2)}) %collective-permute-start.10) | collective-permute-done | bytes 589856 | tf_op jit(solution)/shard_map/ppermute | solution.py:12
  963.0 15.3 %collective-permute-done.11 = bf16[192,1536]{1,0:T(8,128)(2,1)S(1)} collective-permute-done((bf16[192,1536]{1,0:T(8,128)(2,1)S(1)}, bf16[192,1536]{1,0:T(8,128)(2,1)S(1)}, u32[]{:S(2)}, u32[]{:S(2)}) %collective-permute-start.11) | collective-permute-done | bytes 589856 | tf_op jit(solution)/shard_map/ppermute | solution.py:12
  986.0 9.5 collective-permute-done.12
  1003.5 8.6 collective-permute-done.13
  1013.1 7.0 fusion.1
  1030.7 7.9 psum.7
  (203 shorter events, 259.6 us)
Async XLA Ops:
  7.2 85.0 %all-gather.12.cloned.1.call-start = ((), (), s32[]{:S(2)}) async-start(), calls=%async_computation.3 | async-start | bytes 5308416 | tf_op jit(solution)/shard_map/all_gather | solution.py:35
  7.9 288.4 %all-gather.8.cloned.1.call-start = ((), (), s32[]{:S(2)}) async-start(), calls=%async_computation.1 | async-start | bytes 5308416 | tf_op jit(solution)/shard_map/all_gather | solution.py:35
  96.5 126.1 %copy-start.6 = (bf16[384,1536]{1,0:T(8,128)(2,1)}, bf16[384,1536]{1,0:T(8,128)(2,1)S(1)}, u32[]{:S(2)}) copy-start(bf16[384,1536]{1,0:T(8,128)(2,1)S(1)} %fusion.7) | copy-start | bytes 3538948
  97.8 14.3 %collective-permute-start = (bf16[192,1536]{1,0:T(8,128)(2,1)S(1)}, bf16[192,1536]{1,0:T(8,128)(2,1)S(1)}, u32[]{:S(2)}, u32[]{:S(2)}) collective-permute-start(bf16[192,1536]{1,0:T(8,128)(2,1)S(1)} %get-tuple-element.28), channel_id=1, source_target_pairs={{0,7},{1,0},{2,1},{3,2},{4,3},{5,4},{6,5},{7,6},{8,15},{9,8},{10,9... | collective-permute-start | bytes 1769480 | tf_op jit(solution)/shard_map/ppermute | solution.py:12
  112.1 16.9 %collective-permute-start.1 = (bf16[192,1536]{1,0:T(8,128)(2,1)S(1)}, bf16[192,1536]{1,0:T(8,128)(2,1)S(1)}, u32[]{:S(2)}, u32[]{:S(2)}) collective-permute-start(bf16[192,1536]{1,0:T(8,128)(2,1)S(1)} %collective-permute-done), channel_id=1, source_target_pairs={{0,7},{1,0},{2,1},{3,2},{4,3},{5,4},{6,5},{7,6},{8,15},{9,8},{10,9... | collective-permute-start | bytes 1769480 | tf_op jit(solution)/shard_map/ppermute | solution.py:12
  129.0 16.1 %collective-permute-start.2 = (bf16[192,1536]{1,0:T(8,128)(2,1)S(1)}, bf16[192,1536]{1,0:T(8,128)(2,1)S(1)}, u32[]{:S(2)}, u32[]{:S(2)}) collective-permute-start(bf16[192,1536]{1,0:T(8,128)(2,1)S(1)} %collective-permute-done.1), channel_id=1, source_target_pairs={{0,7},{1,0},{2,1},{3,2},{4,3},{5,4},{6,5},{7,6},{8,15},{9,8},{10,9... | collective-permute-start | bytes 1769480 | tf_op jit(solution)/shard_map/ppermute | solution.py:12
  145.1 0.8 copy-start.8
  145.9 15.2 %collective-permute-start.3 = (bf16[192,1536]{1,0:T(8,128)(2,1)S(1)}, bf16[192,1536]{1,0:T(8,128)(2,1)}, u32[]{:S(2)}, u32[]{:S(2)}) collective-permute-start(bf16[192,1536]{1,0:T(8,128)(2,1)S(1)} %collective-permute-done.2), channel_id=1, source_target_pairs={{0,7},{1,0},{2,1},{3,2},{4,3},{5,4},{6,5},{7,6},{8,15},{9,8},{10,9... | collective-permute-start | bytes 1769480 | tf_op jit(solution)/shard_map/ppermute | solution.py:12
  161.1 14.8 %collective-permute-start.4 = (bf16[192,1536]{1,0:T(8,128)(2,1)}, bf16[192,1536]{1,0:T(8,128)(2,1)}, u32[]{:S(2)}, u32[]{:S(2)}) collective-permute-start(bf16[192,1536]{1,0:T(8,128)(2,1)} %collective-permute-done.3), channel_id=1, source_target_pairs={{0,7},{1,0},{2,1},{3,2},{4,3},{5,4},{6,5},{7,6},{8,15},{9,8},{10,9... | collective-permute-start | bytes 1769480 | tf_op jit(solution)/shard_map/ppermute | solution.py:12
  166.4 16.4 %copy-start.9 = (bf16[192,1536]{1,0:T(8,128)(2,1)S(1)}, bf16[192,1536]{1,0:T(8,128)(2,1)}, u32[]{:S(2)}) copy-start(bf16[192,1536]{1,0:T(8,128)(2,1)} %copy-done.8) | copy-start | bytes 1769476
  175.9 13.8 %collective-permute-start.5 = (bf16[192,1536]{1,0:T(8,128)(2,1)}, bf16[192,1536]{1,0:T(8,128)(2,1)S(1)}, u32[]{:S(2)}, u32[]{:S(2)}) collective-permute-start(bf16[192,1536]{1,0:T(8,128)(2,1)} %collective-permute-done.4), channel_id=1, source_target_pairs={{0,7},{1,0},{2,1},{3,2},{4,3},{5,4},{6,5},{7,6},{8,15},{9,8},{10,9... | collective-permute-start | bytes 1769480 | tf_op jit(solution)/shard_map/ppermute | solution.py:12
  189.8 12.5 %collective-permute-start.6 = (bf16[192,1536]{1,0:T(8,128)(2,1)S(1)}, bf16[192,1536]{1,0:T(8,128)(2,1)S(1)}, u32[]{:S(2)}, u32[]{:S(2)}) collective-permute-start(bf16[192,1536]{1,0:T(8,128)(2,1)S(1)} %collective-permute-done.5), channel_id=1, source_target_pairs={{0,7},{1,0},{2,1},{3,2},{4,3},{5,4},{6,5},{7,6},{8,15},{9,8},{10,9... | collective-permute-start | bytes 1769480 | tf_op jit(solution)/shard_map/ppermute | solution.py:12
  203.2 9.4 copy-start.12
  210.4 2.2 copy-start.1
  212.6 3.8 copy-start.10
  215.1 809.3 %all-gather.6.cloned.1.call-start = ((), (), s32[]{:S(2)}) async-start(), calls=%async_computation | async-start | bytes 5308416 | tf_op jit(solution)/shard_map/all_gather | solution.py:40
  215.8 828.4 %all-gather.10.cloned.1.call-start = ((), (), s32[]{:S(2)}) async-start(), calls=%async_computation.2 | async-start | bytes 5308416 | tf_op jit(solution)/shard_map/all_gather | solution.py:40
  216.4 6.2 copy-start.2
  317.1 3.6 copy-start
  648.1 171.2 %copy-start.3 = (f32[392,1536]{1,0:T(8,128)S(1)}, f32[392,1536]{1,0:T(8,128)}, u32[]{:S(2)}) copy-start(f32[392,1536]{1,0:T(8,128)} %pad_maximum_fusion) | copy-start | bytes 7225348
  819.3 2.8 copy-start.7
  850.6 1.8 copy-start.5
  852.4 27.1 %collective-permute-start.7 = (bf16[192,1536]{1,0:T(8,128)(2,1)S(1)}, bf16[192,1536]{1,0:T(8,128)(2,1)S(1)}, u32[]{:S(2)}, u32[]{:S(2)}) collective-permute-start(bf16[192,1536]{1,0:T(8,128)(2,1)S(1)} %get-tuple-element.25), channel_id=1, source_target_pairs={{0,7},{1,0},{2,1},{3,2},{4,3},{5,4},{6,5},{7,6},{8,15},{9,8},{10,9... | collective-permute-start | bytes 1769480 | tf_op jit(solution)/shard_map/ppermute | solution.py:12
  879.6 18.7 %collective-permute-start.8 = (bf16[192,1536]{1,0:T(8,128)(2,1)S(1)}, bf16[192,1536]{1,0:T(8,128)(2,1)S(1)}, u32[]{:S(2)}, u32[]{:S(2)}) collective-permute-start(bf16[192,1536]{1,0:T(8,128)(2,1)S(1)} %collective-permute-done.7), channel_id=1, source_target_pairs={{0,7},{1,0},{2,1},{3,2},{4,3},{5,4},{6,5},{7,6},{8,15},{9,8},{10,9... | collective-permute-start | bytes 1769480 | tf_op jit(solution)/shard_map/ppermute | solution.py:12
  898.3 33.1 %collective-permute-start.9 = (bf16[192,1536]{1,0:T(8,128)(2,1)S(1)}, bf16[192,1536]{1,0:T(8,128)(2,1)S(1)}, u32[]{:S(2)}, u32[]{:S(2)}) collective-permute-start(bf16[192,1536]{1,0:T(8,128)(2,1)S(1)} %collective-permute-done.8), channel_id=1, source_target_pairs={{0,7},{1,0},{2,1},{3,2},{4,3},{5,4},{6,5},{7,6},{8,15},{9,8},{10,9... | collective-permute-start | bytes 1769480 | tf_op jit(solution)/shard_map/ppermute | solution.py:12
  931.4 31.4 %collective-permute-start.10 = (bf16[192,1536]{1,0:T(8,128)(2,1)S(1)}, bf16[192,1536]{1,0:T(8,128)(2,1)S(1)}, u32[]{:S(2)}, u32[]{:S(2)}) collective-permute-start(bf16[192,1536]{1,0:T(8,128)(2,1)S(1)} %collective-permute-done.9), channel_id=1, source_target_pairs={{0,7},{1,0},{2,1},{3,2},{4,3},{5,4},{6,5},{7,6},{8,15},{9,8},{10,9... | collective-permute-start | bytes 1769480 | tf_op jit(solution)/shard_map/ppermute | solution.py:12
  962.8 15.4 %collective-permute-start.11 = (bf16[192,1536]{1,0:T(8,128)(2,1)S(1)}, bf16[192,1536]{1,0:T(8,128)(2,1)S(1)}, u32[]{:S(2)}, u32[]{:S(2)}) collective-permute-start(bf16[192,1536]{1,0:T(8,128)(2,1)S(1)} %collective-permute-done.10), channel_id=1, source_target_pairs={{0,7},{1,0},{2,1},{3,2},{4,3},{5,4},{6,5},{7,6},{8,15},{9,8},{10,9... | collective-permute-start | bytes 1769480 | tf_op jit(solution)/shard_map/ppermute | solution.py:12
  978.3 17.3 %collective-permute-start.12 = (bf16[192,1536]{1,0:T(8,128)(2,1)S(1)}, bf16[192,1536]{1,0:T(8,128)(2,1)S(1)}, u32[]{:S(2)}, u32[]{:S(2)}) collective-permute-start(bf16[192,1536]{1,0:T(8,128)(2,1)S(1)} %collective-permute-done.11), channel_id=1, source_target_pairs={{0,7},{1,0},{2,1},{3,2},{4,3},{5,4},{6,5},{7,6},{8,15},{9,8},{10,9... | collective-permute-start | bytes 1769480 | tf_op jit(solution)/shard_map/ppermute | solution.py:12
  995.5 16.6 %collective-permute-start.13 = (bf16[192,1536]{1,0:T(8,128)(2,1)S(1)}, bf16[192,1536]{1,0:T(8,128)(2,1)S(1)}, u32[]{:S(2)}, u32[]{:S(2)}) collective-permute-start(bf16[192,1536]{1,0:T(8,128)(2,1)S(1)} %collective-permute-done.12), channel_id=1, source_target_pairs={{0,7},{1,0},{2,1},{3,2},{4,3},{5,4},{6,5},{7,6},{8,15},{9,8},{10,9... | collective-permute-start | bytes 1769480 | tf_op jit(solution)/shard_map/ppermute | solution.py:12
  1020.1 2.7 copy-start.4
  1022.9 15.8 %copy-start.11 = (f32[8,8]{1,0:T(8,128)S(1)}, f32[8,8]{1,0:T(8,128)}, u32[]{:S(2)}) copy-start(f32[8,8]{1,0:T(8,128)} %param.11) | copy-start | bytes 772
  1022.9 25.8 %collective-permute-start.14 = (f32[192,1536]{1,0:T(8,128)}, f32[192,1536]{1,0:T(8,128)S(1)}, u32[]{:S(2)}, u32[]{:S(2)}) collective-permute-start(f32[192,1536]{1,0:T(8,128)} %fusion.143), channel_id=1, source_target_pairs={{0,8},{8,16},{16,24},{1,9},{9,17},{17,25},{2,10},{10,18},{18,26},{... | collective-permute-start | bytes 3538952 | tf_op jit(solution)/shard_map/ppermute | solution.py:21
Sparse Core Ops, SparseCore 0:
  10.1 82.0 all-gather.11
  215.2 80.9 all-gather.7
  298.4 77.2 all-gather.5
  852.6 116.3 all-gather.9
